TPU v7x, 32 devices: a whole 2x2x4 slice. The times are simulated.
32 devices in a mesh: rows: 16 (over z, y, core), cols: 2 (over x).
Axes of the slice: x: 2, y: 2, z: 4, core: 2. Of those that a mesh axis runs over, the one named last changes fastest.
Arguments:
- features: bfloat16 [4096, 128], P('rows', 'cols'), may hold values from -6 to 6
- adj_tiles: bfloat16 [1536, 128, 128], P('rows'), may hold values from -0.109375 to 0.109375
- tile_src: int32 [1536], P('rows'), may hold values from 0 to 31, as said below
- tile_dst: int32 [1536], P('rows'), may hold values from 0 to 1, as said below
- tile_count: int32 [16], P('rows'), may hold values from 24 to 96, as said below
- cluster_size: int32 [32], P('rows'), may hold values from 64 to 128, as said below
- weight: bfloat16 [128, 256], P(None, 'cols'), may hold values from -0.5 to 0.5
- bias: float32 [256], P('cols'), may hold values from -3 to 3
- grad_out: bfloat16 [4096, 256], P('rows', 'cols'), may hold values from -6 to 6
Outputs:
- hidden: bfloat16 [4096, 256], P('rows', 'cols')
- grad_weight: float32 [128, 256], P(None, 'cols')
- grad_bias: float32 [256], P('cols')
- grad_features: bfloat16 [4096, 128], P('rows', 'cols')
Inputs may be any that keep to these rules, and one draw needn't show every extreme that they name: In row group r, slots 0 to tile_count[r] - 1 of its 96 slots hold tiles, in non-decreasing order of tile_src; the later slots are unused: their tile_src and tile_dst hold 0, and their adj_tiles hold arbitrary values that must not contribute. A used slot's column cluster belongs to row group r itself or to a row group whose index differs from r in exactly one bit (row group g holds clusters g * 2 to g * 2 + 1). Equal (row, column) pairs may repeat and then add. `tile_dst`: unused slots hold 0. `tile_count`: some row groups use all 96 slots. `cluster_size`: the real nodes of a cluster are its first ones; some cluster is full.
All inputs are finite; a program needn't handle non-finite values.
Results may differ from a plain program's by a relative error of at most 0.006.
Values may be sent and summed in bfloat16 or wider, within the bound.
No kernel may reach another device: no remote copies, remote signals or barrier semaphores. Data moves between devices by JAX's collectives and lax.ppermute only.
A program may use at most 64 MiB of HBM per device.

v0:
```python
import math
import jax
import jax.numpy as jnp
from jax import lax
from jax.sharding import PartitionSpec as P

TILE_GROUP = 16


def partner(shard, axis, distance):
    return lax.ppermute(shard, axis, [(i, i ^ 1 << distance) for i in range(lax.axis_size(axis))])


def sweep_slots(first_slot, last_slot, work, totals):
    turn_count = (last_slot - first_slot + TILE_GROUP - 1) // TILE_GROUP

    def one_turn(turn_index, carried):
        slot_ids = first_slot + turn_index * TILE_GROUP + jnp.arange(TILE_GROUP, dtype=jnp.int32)
        return work(carried, slot_ids, slot_ids < last_slot)

    return lax.fori_loop(0, jnp.maximum(turn_count, 0), one_turn, totals)


def slot_bounds(sources, first_slot, last_slot, low_cluster, high_cluster):
    positions = jnp.arange(sources.shape[0], dtype=jnp.int32)
    inside = (positions >= first_slot) & (positions < last_slot)
    below_low = jnp.sum((inside & (sources < low_cluster)).astype(jnp.int32))
    below_high = jnp.sum((inside & (sources < high_cluster)).astype(jnp.int32))
    return (first_slot + below_low, first_slot + below_high)


def neighbour_slots(sources, own_group, per_group, levels):
    group_of = sources // per_group
    within = sources - group_of * per_group
    differs = jnp.bitwise_xor(group_of, own_group)
    level = jnp.zeros_like(sources)
    for bit in range(levels):
        level = level + (bit + 1) * (differs == 1 << bit).astype(jnp.int32)
    return level * per_group + within


def gather_products(
    totals, tile_data, sources, targets, slot_ids, is_valid, row_table, base_cluster
):
    clamped = jnp.minimum(slot_ids, tile_data.shape[0] - 1)
    tile_block = tile_data[clamped]
    from_rows = jnp.clip(sources[clamped] - base_cluster, 0, row_table.shape[0] - 1)
    products = jnp.einsum(
        "tij,tjf->tif", tile_block, row_table[from_rows], preferred_element_type=jnp.float32
    )
    placed = jnp.where(is_valid, targets[clamped], totals.shape[0])
    return totals.at[placed].add(products, mode="drop")


def spread_products(
    totals, tile_data, sources, targets, slot_ids, is_valid, grad_table, base_cluster
):
    clamped = jnp.minimum(slot_ids, tile_data.shape[0] - 1)
    tile_block = tile_data[clamped]
    products = jnp.einsum(
        "tji,tjf->tif", tile_block, grad_table[targets[clamped]], preferred_element_type=jnp.float32
    )
    placed = jnp.where(is_valid, sources[clamped] - base_cluster, totals.shape[0])
    return totals.at[placed].add(products, mode="drop")


def local(
    features, adj_tiles, tile_src, tile_dst, tile_count, cluster_size, weight, bias, grad_out
):
    clusters_here = cluster_size.shape[0]
    tile_width = adj_tiles.shape[1]
    feat_half = features.shape[1]
    node_rows = clusters_here * tile_width
    node_ids = jnp.arange(tile_width, dtype=jnp.int32)
    live_node = (node_ids[None, :] < cluster_size[:, None]).astype(jnp.float32)[:, :, None]
    live_flat = live_node.reshape(node_rows, 1)
    masked = (
        features.reshape(clusters_here, tile_width, feat_half).astype(jnp.float32) * live_node
    ).astype(jnp.bfloat16)
    my_count = tile_count[0]
    levels = lax.axis_size("rows").bit_length() - 1
    local_slots = neighbour_slots(tile_src, lax.axis_index("rows"), clusters_here, levels)
    zero_totals = jnp.zeros((clusters_here, tile_width, feat_half), jnp.float32)
    whole_rows = lax.all_gather(masked, "rows", axis=0, tiled=True)
    row_count = whole_rows.shape[0]
    first_slot, last_slot = slot_bounds(tile_src, 0, my_count, 0, 0 + row_count)
    own_totals = sweep_slots(
        first_slot,
        last_slot,
        lambda totals, slot_ids, is_valid: gather_products(
            totals, adj_tiles, tile_src, tile_dst, slot_ids, is_valid, whole_rows, 0
        ),
        zero_totals,
    )
    agg_local = own_totals.reshape(node_rows, feat_half).astype(jnp.bfloat16)
    agg_full = lax.all_gather(agg_local, "cols", axis=1, tiled=True)
    pre_activation = jnp.dot(agg_full, weight, preferred_element_type=jnp.float32) + bias
    sigmoid_pre = jax.nn.sigmoid(pre_activation)
    hidden = (pre_activation * sigmoid_pre * live_flat).astype(jnp.bfloat16)
    grad_pre = (
        grad_out.astype(jnp.float32)
        * sigmoid_pre
        * (1.0 + pre_activation * (1.0 - sigmoid_pre))
        * live_flat
    ).astype(jnp.bfloat16)
    weight_term = lax.dot_general(
        agg_full, grad_pre, (((0,), (0,)), ((), ())), preferred_element_type=jnp.float32
    )
    bias_term = jnp.sum(grad_pre.astype(jnp.float32), axis=0)
    weight_total, bias_total = lax.psum((weight_term, bias_term), "rows")
    grad_scale = 1.0 / math.sqrt(node_rows * lax.axis_size("rows"))
    grad_weight = weight_total * grad_scale
    grad_bias = bias_total * grad_scale
    partial_value = lax.dot_general(
        grad_pre, weight, (((1,), (1,)), ((), ())), preferred_element_type=jnp.float32
    )
    grad_agg = (
        lax.psum_scatter(partial_value, "cols", scatter_dimension=1, tiled=True)
        .astype(jnp.bfloat16)
        .reshape(clusters_here, tile_width, feat_half)
    )
    buckets = jnp.zeros(((levels + 1) * clusters_here, tile_width, feat_half), jnp.float32)
    buckets = sweep_slots(
        0,
        my_count,
        lambda carried, slot_ids, is_valid: spread_products(
            carried, adj_tiles, local_slots, tile_dst, slot_ids, is_valid, grad_agg, 0
        ),
        buckets,
    )
    summed = buckets[:clusters_here]
    for bit in range(levels):
        summed = summed + partner(
            buckets[(bit + 1) * clusters_here : (bit + 2) * clusters_here], "rows", bit
        )
    grad_features = (summed * live_node).reshape(node_rows, feat_half).astype(jnp.bfloat16)
    return (hidden, grad_weight, grad_bias, grad_features)


def solution(mesh):
    return jax.shard_map(
        local,
        mesh=mesh,
        in_specs=(
            P("rows", "cols"),
            P("rows", None, None),
            P("rows"),
            P("rows"),
            P("rows"),
            P("rows"),
            P(None, "cols"),
            P("cols"),
            P("rows", "cols"),
        ),
        out_specs=(P("rows", "cols"), P(None, "cols"), P("cols"), P("rows", "cols")),
        check_vma=False,
    )
```

profile of v0, /device:TPU:8, one launch (start us, length us, event | category | flops | bytes accessed | tf_op | source)
XLA Modules:
  0.0 193.4 jit_solution(5257428830742332566)
XLA Ops:
  12.9 20.3 %all_gather.6 = bf16[32,128,64]{1,2,0:T(8,128)(2,1)S(1)} all-gather(bf16[2,128,64]{1,2,0:T(8,128)(2,1)S(1)} %copy.30), channel_id=1, replica_groups=mesh['rows'=16,'cols'=2] {'rows'}, dimensions={0}, use_global_device_ids=true | all-gather | bytes 557056 | tf_op jit(solution)/shard_map/all_gather | solution.py:84
  33.8 27.2 %while.20 = (s32[]{:T(128)}, f32[2,128,64]{1,2,0:T(8,128)S(1)}, s32[]{:T(128)}, s32[]{:T(128)}, s32[]{:T(128)}, /*index=5*/s32[96]{0:T(128)}, bf16[96,128,128]{2...) while((s32[]{:T(128)}, f32[2,128,64]{1,2,0:T(8,128)S(1)}, ...), condition=%wide.region_4.5_spmd, body=%wide.region_2.4_spmd.sunk | while | flops 33687796 | bytes 4465817 | solution.py:21
  34.5 1.3 gather_fusion
  36.4 2.5 %gather_fusion.1 = bf16[16,128,128]{2,1,0:T(8,128)(2,1)S(1)} fusion(bf16[96,128,128]{2,1,0:T(8,128)(2,1)} %get-tuple-element.328, s32[1024]{0:T(1024)S(1)} %pad_clamp_fusion.8), kind=kCustom, calls=%fused_computation.1.clone.1 | custom fusion | bytes 1048640 | tf_op jit(solution)/shard_map/while/body/gather | solution.py:46
  39.0 1.3 gather_fusion.2
  41.5 1.4 scatter_fusion
  45.5 2.5 %gather_fusion.1 = bf16[16,128,128]{2,1,0:T(8,128)(2,1)S(1)} fusion(bf16[96,128,128]{2,1,0:T(8,128)(2,1)} %get-tuple-element.328, s32[1024]{0:T(1024)S(1)} %pad_clamp_fusion.8), kind=kCustom, calls=%fused_computation.1.clone.1 | custom fusion | bytes 1048640 | tf_op jit(solution)/shard_map/while/body/gather | solution.py:46
  50.5 1.4 scatter_fusion
  54.6 2.5 %gather_fusion.1 = bf16[16,128,128]{2,1,0:T(8,128)(2,1)S(1)} fusion(bf16[96,128,128]{2,1,0:T(8,128)(2,1)} %get-tuple-element.328, s32[1024]{0:T(1024)S(1)} %pad_clamp_fusion.8), kind=kCustom, calls=%fused_computation.1.clone.1 | custom fusion | bytes 1048640 | tf_op jit(solution)/shard_map/while/body/gather | solution.py:46
  59.6 1.4 scatter_fusion
  61.0 4.6 %all_gather.7 = bf16[256,128]{0,1:T(8,128)(2,1)S(1)} all-gather(bf16[256,64]{0,1:T(8,128)(2,1)S(1)} %copy_bitcast_fusion.1), channel_id=1, replica_groups=mesh['rows'=16,'cols'=2] {'cols'}, dimensions={1}, use_global_device_ids=true | all-gather | bytes 98304 | tf_op jit(solution)/shard_map/all_gather | solution.py:96
  68.2 48.7 %psum.15 = f32[128]{0:T(128)S(1)} all-reduce(f32[128]{0:T(128)S(1)} %get-tuple-element.184), channel_id=1, replica_groups=mesh['rows'=16,'cols'=2] {'rows'}, use_global_device_ids=true, to_apply=%region_7.8 | all-reduce | flops 128 | bytes 1024 | tf_op jit(solution)/shard_map/psum | solution.py:110
  118.4 22.8 %while.21 = (s32[]{:T(128)}, f32[10,128,64]{1,2,0:T(8,128)S(1)}, s32[]{:T(128)}, s32[]{:T(128)}, s32[96]{0:T(128)S(1)}, /*index=5*/bf16[96,128,128]{2,1,0:T(8,12...) while((s32[]{:T(128)}, f32[10,128,64]{1,2,0:T(8,128)S(1)}, s32[]{:T(128)}, ...), condition=%wide.region_11.12_spmd, body=%wide.region_9.11_spmd.sunk | while | flops 33687776 | bytes 4465797 | solution.py:21
  119.8 2.5 %gather_fusion.5 = bf16[16,128,128]{2,1,0:T(8,128)(2,1)S(1)} fusion(bf16[96,128,128]{2,1,0:T(8,128)(2,1)} %get-tuple-element.358, s32[1024]{0:T(1024)S(1)} %pad_clamp_fusion.10), kind=kCustom, calls=%fused_computation.5.clone.1 | custom fusion | bytes 1048640 | tf_op jit(solution)/shard_map/while/body/gather | solution.py:59
  122.3 1.3 gather_fusion.6
  124.6 1.3 scatter_fusion.1
  127.4 2.5 %gather_fusion.5 = bf16[16,128,128]{2,1,0:T(8,128)(2,1)S(1)} fusion(bf16[96,128,128]{2,1,0:T(8,128)(2,1)} %get-tuple-element.358, s32[1024]{0:T(1024)S(1)} %pad_clamp_fusion.10), kind=kCustom, calls=%fused_computation.5.clone.1 | custom fusion | bytes 1048640 | tf_op jit(solution)/shard_map/while/body/gather | solution.py:59
  132.2 1.4 scatter_fusion.1
  134.9 2.6 %gather_fusion.5 = bf16[16,128,128]{2,1,0:T(8,128)(2,1)S(1)} fusion(bf16[96,128,128]{2,1,0:T(8,128)(2,1)} %get-tuple-element.358, s32[1024]{0:T(1024)S(1)} %pad_clamp_fusion.10), kind=kCustom, calls=%fused_computation.5.clone.1 | custom fusion | bytes 1048640 | tf_op jit(solution)/shard_map/while/body/gather | solution.py:59
  137.5 1.3 gather_fusion.6
  139.8 1.3 scatter_fusion.1
  141.6 23.7 %collective-permute-start.2 = (f32[2,128,64]{1,0,2:T(2,128)S(1)}, f32[2,128,64]{1,0,2:T(2,128)S(1)}, u32[]{:S(2)}, u32[]{:S(2)}) collective-permute-start(f32[2,128,64]{1,0,2:T(2,128)S(1)} %get-tuple-element.188), channel_id=1, source_target_pairs={{0,8},{2,10},{4,12},{6,14},{8,0},{10,2},{12,4},{14,6},{16,24},{18,... | collective-permute-start | bytes 196616 | tf_op jit(solution)/shard_map/ppermute | solution.py:11
  165.2 18.5 %all-reduce.2.cloned.1.call-done = f32[128,128]{1,0:T(8,128)} async-done(((f32[128,128]{1,0:T(8,128)}), f32[128,128]{1,0:T(8,128)}) %all-reduce.2.cloned.1.call-update) | async-done | bytes 65552 | tf_op jit(solution)/shard_map/psum | solution.py:110
  183.7 1.5 broadcast_multiply_fusion
  (87 shorter events, 27.5 us)
Async XLA Ops:
  8.0 57.6 %copy-start = (bf16[128,128]{1,0:T(8,128)(2,1)S(1)}, bf16[128,128]{1,0:T(8,128)(2,1)}, u32[]{:S(2)}) copy-start(bf16[128,128]{1,0:T(8,128)(2,1)} %param.19) | copy-start | bytes 98308
  8.0 109.4 %reduce-scatter.2.cloned.1.call-start = ((), (), s32[]{:S(2)}) async-start(), calls=%async_computation.2 | async-start | bytes 196608 | tf_op jit(solution)/shard_map/reduce_scatter | solution.py:118
  33.7 31.8 %copy-start.1 = (bf16[256,128]{1,0:T(8,128)(2,1)S(1)}, bf16[256,128]{1,0:T(8,128)(2,1)}, u32[]{:S(2)}) copy-start(bf16[256,128]{1,0:T(8,128)(2,1)} %param.21) | copy-start | bytes 196612
  33.7 31.8 %copy-start.2 = (f32[128]{0:T(128)S(1)}, f32[128]{0:T(128)}, u32[]{:S(2)}) copy-start(f32[128]{0:T(128)} %param.20) | copy-start | bytes 1540
  67.3 116.4 %all-reduce.2.cloned.1.call-start = ((), (), s32[]{:S(2)}) async-start(), calls=%async_computation.1 | async-start | bytes 131072 | tf_op jit(solution)/shard_map/psum | solution.py:110
  141.5 43.7 %collective-permute-start.3 = (f32[2,128,64]{1,0,2:T(2,128)S(1)}, f32[2,128,64]{1,0,2:T(2,128)S(1)}, u32[]{:S(2)}, u32[]{:S(2)}) collective-permute-start(f32[2,128,64]{1,0,2:T(2,128)S(1)} %get-tuple-element.187), channel_id=1, source_target_pairs={{0,16},{2,18},{4,20},{6,22},{8,24},{10,26},{12,28},{14,30},{16,0},... | collective-permute-start | bytes 196616 | tf_op jit(solution)/shard_map/ppermute | solution.py:11
  141.6 43.6 %collective-permute-start.2 = (f32[2,128,64]{1,0,2:T(2,128)S(1)}, f32[2,128,64]{1,0,2:T(2,128)S(1)}, u32[]{:S(2)}, u32[]{:S(2)}) collective-permute-start(f32[2,128,64]{1,0,2:T(2,128)S(1)} %get-tuple-element.188), channel_id=1, source_target_pairs={{0,8},{2,10},{4,12},{6,14},{8,0},{10,2},{12,4},{14,6},{16,24},{18,... | collective-permute-start | bytes 196616 | tf_op jit(solution)/shard_map/ppermute | solution.py:11
  165.2 20.0 %collective-permute-start.1 = (f32[2,128,64]{1,0,2:T(2,128)S(1)}, f32[2,128,64]{1,0,2:T(2,128)S(1)}, u32[]{:S(2)}, u32[]{:S(2)}) collective-permute-start(f32[2,128,64]{1,0,2:T(2,128)S(1)} %get-tuple-element.189), channel_id=1, source_target_pairs={{0,4},{2,6},{4,0},{6,2},{8,12},{10,14},{12,8},{14,10},{16,20},{18,... | collective-permute-start | bytes 196616 | tf_op jit(solution)/shard_map/ppermute | solution.py:11
  165.2 20.0 %collective-permute-start = (f32[2,128,64]{1,0,2:T(2,128)S(1)}, f32[2,128,64]{1,0,2:T(2,128)S(1)}, u32[]{:S(2)}, u32[]{:S(2)}) collective-permute-start(f32[2,128,64]{1,0,2:T(2,128)S(1)} %get-tuple-element.186), channel_id=1, source_target_pairs={{0,2},{2,0},{4,6},{6,4},{8,10},{10,8},{12,14},{14,12},{16,18},{18,... | collective-permute-start | bytes 196616 | tf_op jit(solution)/shard_map/ppermute | solution.py:11
Sparse Core Ops, SparseCore 0:
  67.4 33.8 reduce-scatter.1
Sparse Core Ops, SparseCore 1:
  71.8 111.9 all-reduce.1
where the time goes:
time: 195 us; the launch traced here: 193 us
  blocking collectives  73.6 us (38%)
  local copies, waits for them, and re-layouts  35.4 us (18%)
  starting transfers between devices  23.8 us (12%)
  waiting for transfers between devices  18.5 us (9%)
  between operations  17.6 us (9%)
  other arithmetic  17.2 us (9%)
  matrix products  4.85 us (2%)
  loops' own time  2.36 us (1%)
    psum x1, blocking collectives, local(): weight_total, bias_total = lax.psum((weight_term, bias_term), 'rows')  48.7 us
    ppermute x4, starting transfers between devices, partner(): lax.ppermute(shard, axis, [(i, i ^ 1 << distance) for i in range(lax.axis...  23.7 us
    all_gather x1, blocking collectives, local(): whole_rows = lax.all_gather(masked, 'rows', axis=0, tiled=True)  20.3 us
    psum x1, waiting for transfers between devices, local(): weight_total, bias_total = lax.psum((weight_term, bias_term), 'rows')  18.5 us
    gather x3, local copies, waits for them, and re-layouts, spread_products(): tile_block = tile_data[clamped]  7.64 us
    gather x3, local copies, waits for them, and re-layouts, gather_products(): tile_block = tile_data[clamped]  7.62 us
    all_gather x1, blocking collectives, local(): agg_full = lax.all_gather(agg_local, 'cols', axis=1, tiled=True)  4.58 us
    scatter-add x3, other arithmetic, gather_products(): return totals.at[placed].add(products, mode='drop')  4.07 us
  transfers between devices with their start and end apart: 6, of which 1 were waited for; matrix products, arithmetic and copies ran while one was open for 14% of the time, Pallas kernels for 0%

commit v1 on v0

--- a/solution.py
+++ b/solution.py
@@ -5,6 +5,17 @@
 from jax.sharding import PartitionSpec as P
 
 TILE_GROUP = 16
+
+
+def gather_around(value, axis, dim):
+    ways = lax.axis_size(axis)
+    pieces = [value]
+    for far in range(1, ways):
+        pieces.append(
+            lax.ppermute(pieces[far - 1], axis, [(d, (d - 1) % ways) for d in range(ways)])
+        )
+    line = jnp.concatenate(pieces, axis=dim)
+    return jnp.roll(line, lax.axis_index(axis) * value.shape[dim], axis=dim)
 
 
 def partner(shard, axis, distance):
@@ -81,7 +92,7 @@
     levels = lax.axis_size("rows").bit_length() - 1
     local_slots = neighbour_slots(tile_src, lax.axis_index("rows"), clusters_here, levels)
     zero_totals = jnp.zeros((clusters_here, tile_width, feat_half), jnp.float32)
-    whole_rows = lax.all_gather(masked, "rows", axis=0, tiled=True)
+    whole_rows = gather_around(masked, "rows", 0)
     row_count = whole_rows.shape[0]
     first_slot, last_slot = slot_bounds(tile_src, 0, my_count, 0, 0 + row_count)
     own_totals = sweep_slots(

time: 195 us -> 269 us (1.38)
  starting transfers between devices: 23.8 us -> 73 us
  waiting for transfers between devices: 18.5 us -> 67.3 us
  blocking collectives: 73.6 us -> 54.1 us
  local copies, waits for them, and re-layouts: 35.4 us -> 31.8 us
    ppermute x0 -> x15, starting transfers between devices: none -> 49.1 us  [gather_around(): lax.ppermute(pieces[far - 1], axis, [(d, (d - 1) % ways) for d in range(w...]
    ppermute x0 -> x15, waiting for transfers between devices: none -> 21.7 us  [gather_around(): lax.ppermute(pieces[far - 1], axis, [(d, (d - 1) % ways) for d in range(w...]
    all_gather x1 -> x0, blocking collectives: 20.3 us -> none  [local(): whole_rows = lax.all_gather(masked, 'rows', axis=0, tiled=True)]
    psum x1, waiting for transfers between devices: 18.5 us -> 36.5 us  [local(): weight_total, bias_total = lax.psum((weight_term, bias_term), 'rows')]
    reduce_scatter x1, waiting for transfers between devices: 0.01 us -> 9.06 us  [local(): lax.psum_scatter(partial_value, 'cols', scatter_dimension=1, tiled=True)]
  transfers between devices with their start and end apart: 6 -> 21, of which waited for: 1 -> 16; matrix products, arithmetic and copies ran while one was open for 14% -> 10% of each run, Pallas kernels for 0% -> 0%
where the time goes in v1:
time: 269 us; the launch traced here: 268 us
  starting transfers between devices  73 us (27%)
  waiting for transfers between devices  67.3 us (25%)
  blocking collectives  54.1 us (20%)
  local copies, waits for them, and re-layouts  31.8 us (12%)
  between operations  17.7 us (7%)
  other arithmetic  17.2 us (6%)
  matrix products  4.86 us (2%)
    psum x1, blocking collectives, local(): weight_total, bias_total = lax.psum((weight_term, bias_term), 'rows')  49.5 us
    ppermute x15, starting transfers between devices, gather_around(): lax.ppermute(pieces[far - 1], axis, [(d, (d - 1) % ways) for d in range(w...  49.1 us
    psum x1, waiting for transfers between devices, local(): weight_total, bias_total = lax.psum((weight_term, bias_term), 'rows')  36.5 us
    ppermute x4, starting transfers between devices, partner(): lax.ppermute(shard, axis, [(i, i ^ 1 << distance) for i in range(lax.axis...  23.8 us
    ppermute x15, waiting for transfers between devices, gather_around(): lax.ppermute(pieces[far - 1], axis, [(d, (d - 1) % ways) for d in range(w...  21.7 us
    reduce_scatter x1, waiting for transfers between devices, local(): lax.psum_scatter(partial_value, 'cols', scatter_dimension=1, tiled=True)  9.06 us
    gather x3, local copies, waits for them, and re-layouts, spread_products(): tile_block = tile_data[clamped]  7.66 us
    gather x3, local copies, waits for them, and re-layouts, gather_products(): tile_block = tile_data[clamped]  7.62 us
  transfers between devices with their start and end apart: 21, of which 16 were waited for; matrix products, arithmetic and copies ran while one was open for 10% of the time, Pallas kernels for 0%

profile of v1, /device:TPU:8, one launch (start us, length us, event | category | flops | bytes accessed | tf_op | source)
XLA Modules:
  0.0 268.2 jit_solution(9060099925468414014)
XLA Ops:
  12.1 2.6 collective-permute-start.1
  16.4 2.6 collective-permute-start.2
  20.6 2.6 collective-permute-start.3
  24.9 2.6 collective-permute-start.4
  29.1 2.6 collective-permute-start.5
  33.3 2.6 collective-permute-start.6
  37.6 2.6 collective-permute-start.7
  41.8 3.1 %collective-permute-start.8 = (bf16[2,128,64]{1,0,2:T(2,128)(2,1)S(1)}, bf16[2,128,64]{1,0,2:T(2,128)(2,1)S(1)}, u32[]{:S(2)}, u32[]{:S(2)}) collective-permute-start(bf16[2,128,64]{1,0,2:T(2,128)(2,1)S(1)} %collective-permute-done.7), channel_id=1, source_target_pairs={{0,30},{2,0},{4,2},{6,4},{8,6},{10,8},{12,10},{14,12},{16,14},{18,... | collective-permute-start | bytes 98312 | tf_op jit(solution)/shard_map/ppermute | solution.py:15
  46.5 4.4 %collective-permute-start.9 = (bf16[2,128,64]{1,0,2:T(2,128)(2,1)S(1)}, bf16[2,128,64]{1,0,2:T(2,128)(2,1)S(1)}, u32[]{:S(2)}, u32[]{:S(2)}) collective-permute-start(bf16[2,128,64]{1,0,2:T(2,128)(2,1)S(1)} %collective-permute-done.8), channel_id=1, source_target_pairs={{0,30},{2,0},{4,2},{6,4},{8,6},{10,8},{12,10},{14,12},{16,14},{18,... | collective-permute-start | bytes 98312 | tf_op jit(solution)/shard_map/ppermute | solution.py:15
  52.5 4.4 %collective-permute-start.10 = (bf16[2,128,64]{1,0,2:T(2,128)(2,1)S(1)}, bf16[2,128,64]{1,0,2:T(2,128)(2,1)S(1)}, u32[]{:S(2)}, u32[]{:S(2)}) collective-permute-start(bf16[2,128,64]{1,0,2:T(2,128)(2,1)S(1)} %collective-permute-done.9), channel_id=1, source_target_pairs={{0,30},{2,0},{4,2},{6,4},{8,6},{10,8},{12,10},{14,12},{16,14},{18,... | collective-permute-start | bytes 98312 | tf_op jit(solution)/shard_map/ppermute | solution.py:15
  58.6 4.4 %collective-permute-start.11 = (bf16[2,128,64]{1,0,2:T(2,128)(2,1)S(1)}, bf16[2,128,64]{1,0,2:T(2,128)(2,1)S(1)}, u32[]{:S(2)}, u32[]{:S(2)}) collective-permute-start(bf16[2,128,64]{1,0,2:T(2,128)(2,1)S(1)} %collective-permute-done.10), channel_id=1, source_target_pairs={{0,30},{2,0},{4,2},{6,4},{8,6},{10,8},{12,10},{14,12},{16,14},{18,... | collective-permute-start | bytes 98312 | tf_op jit(solution)/shard_map/ppermute | solution.py:15
  64.6 4.4 %collective-permute-start.12 = (bf16[2,128,64]{1,0,2:T(2,128)(2,1)S(1)}, bf16[2,128,64]{1,0,2:T(2,128)(2,1)S(1)}, u32[]{:S(2)}, u32[]{:S(2)}) collective-permute-start(bf16[2,128,64]{1,0,2:T(2,128)(2,1)S(1)} %collective-permute-done.11), channel_id=1, source_target_pairs={{0,30},{2,0},{4,2},{6,4},{8,6},{10,8},{12,10},{14,12},{16,14},{18,... | collective-permute-start | bytes 98312 | tf_op jit(solution)/shard_map/ppermute | solution.py:15
  70.6 4.4 %collective-permute-start.13 = (bf16[2,128,64]{1,0,2:T(2,128)(2,1)S(1)}, bf16[2,128,64]{1,0,2:T(2,128)(2,1)S(1)}, u32[]{:S(2)}, u32[]{:S(2)}) collective-permute-start(bf16[2,128,64]{1,0,2:T(2,128)(2,1)S(1)} %collective-permute-done.12), channel_id=1, source_target_pairs={{0,30},{2,0},{4,2},{6,4},{8,6},{10,8},{12,10},{14,12},{16,14},{18,... | collective-permute-start | bytes 98312 | tf_op jit(solution)/shard_map/ppermute | solution.py:15
  76.7 4.4 %collective-permute-start.14 = (bf16[2,128,64]{1,0,2:T(2,128)(2,1)S(1)}, bf16[2,128,64]{1,0,2:T(2,128)(2,1)S(1)}, u32[]{:S(2)}, u32[]{:S(2)}) collective-permute-start(bf16[2,128,64]{1,0,2:T(2,128)(2,1)S(1)} %collective-permute-done.13), channel_id=1, source_target_pairs={{0,30},{2,0},{4,2},{6,4},{8,6},{10,8},{12,10},{14,12},{16,14},{18,... | collective-permute-start | bytes 98312 | tf_op jit(solution)/shard_map/ppermute | solution.py:15
  86.7 23.2 %while.20 = (s32[]{:T(128)}, f32[2,128,64]{1,2,0:T(8,128)S(1)}, s32[]{:T(128)}, s32[]{:T(128)}, s32[]{:T(128)}, /*index=5*/s32[96]{0:T(128)S(1)}, bf16[96,128,12...) while((s32[]{:T(128)}, f32[2,128,64]{1,2,0:T(8,128)S(1)}, ...), condition=%wide.region_4.5_spmd, body=%wide.region_2.4_spmd.sunk | while | flops 33687796 | bytes 4465817 | solution.py:32
  109.9 4.6 %all_gather.3 = bf16[256,128]{0,1:T(8,128)(2,1)S(1)} all-gather(bf16[256,64]{0,1:T(8,128)(2,1)S(1)} %copy_bitcast_fusion.1), channel_id=1, replica_groups=mesh['rows'=16,'cols'=2] {'cols'}, dimensions={1}, use_global_device_ids=true | all-gather | bytes 98304 | tf_op jit(solution)/shard_map/all_gather | solution.py:107
  115.4 49.5 %psum.15 = f32[128]{0:T(128)S(1)} all-reduce(f32[128]{0:T(128)S(1)} %get-tuple-element.167), channel_id=1, replica_groups=mesh['rows'=16,'cols'=2] {'rows'}, use_global_device_ids=true, to_apply=%region_7.8 | all-reduce | flops 128 | bytes 1024 | tf_op jit(solution)/shard_map/psum | solution.py:121
  167.1 9.1 %reduce-scatter.2.cloned.1.call-done = f32[256,64]{0,1:T(8,128)} async-done(((f32[256,128]{0,1:T(8,128)}), f32[256,64]{0,1:T(8,128)}) %reduce-scatter.2.cloned.1.call-update) | async-done | bytes 65552 | tf_op jit(solution)/shard_map/reduce_scatter | solution.py:129
  177.2 20.8 %while.21 = (s32[]{:T(128)}, f32[10,128,64]{1,2,0:T(8,128)S(1)}, s32[]{:T(128)}, s32[]{:T(128)}, s32[96]{0:T(128)S(1)}, /*index=5*/bf16[96,128,128]{2,1,0:T(8,12...) while((s32[]{:T(128)}, f32[10,128,64]{1,2,0:T(8,128)S(1)}, s32[]{:T(128)}, ...), condition=%wide.region_11.12_spmd, body=%wide.region_9.11_spmd.sunk | while | flops 33687776 | bytes 4465797 | solution.py:32
  178.6 2.6 gather_fusion.5
  185.5 2.6 gather_fusion.5
  192.5 2.6 gather_fusion.5
  200.8 21.3 %collective-permute-start.17 = (f32[2,128,64]{1,0,2:T(2,128)S(1)}, f32[2,128,64]{1,0,2:T(2,128)S(1)}, u32[]{:S(2)}, u32[]{:S(2)}) collective-permute-start(f32[2,128,64]{1,0,2:T(2,128)S(1)} %get-tuple-element.171), channel_id=1, source_target_pairs={{0,8},{2,10},{4,12},{6,14},{8,0},{10,2},{12,4},{14,6},{16,24},{18,... | collective-permute-start | bytes 196616 | tf_op jit(solution)/shard_map/ppermute | solution.py:22
  222.1 36.5 %all-reduce.2.cloned.1.call-done = f32[128,128]{1,0:T(8,128)} async-done(((f32[128,128]{1,0:T(8,128)}), f32[128,128]{1,0:T(8,128)}) %all-reduce.2.cloned.1.call-update) | async-done | bytes 65552 | tf_op jit(solution)/shard_map/psum | solution.py:121
  (121 shorter events, 71.4 us)
Async XLA Ops:
  8.0 106.5 %copy-start = (bf16[128,128]{1,0:T(8,128)(2,1)S(1)}, bf16[128,128]{1,0:T(8,128)(2,1)}, u32[]{:S(2)}) copy-start(bf16[128,128]{1,0:T(8,128)(2,1)} %param.19) | copy-start | bytes 98308
  8.0 78.6 %copy-start.2 = (s32[96]{0:T(128)S(1)}, s32[96]{0:T(128)}, u32[]{:S(2)}) copy-start(s32[96]{0:T(128)} %param.15) | copy-start | bytes 1156
  8.0 78.6 %copy-start.1 = (s32[96]{0:T(128)S(1)}, s32[96]{0:T(128)}, u32[]{:S(2)}) copy-start(s32[96]{0:T(128)} %param.16) | copy-start | bytes 1156
  8.0 168.2 %reduce-scatter.2.cloned.1.call-start = ((), (), s32[]{:S(2)}) async-start(), calls=%async_computation.2 | async-start | bytes 196608 | tf_op jit(solution)/shard_map/reduce_scatter | solution.py:129
  9.6 2.5 collective-permute-start
  12.1 4.2 %collective-permute-start.1 = (bf16[2,128,64]{1,0,2:T(2,128)(2,1)S(1)}, bf16[2,128,64]{1,0,2:T(2,128)(2,1)S(1)}, u32[]{:S(2)}, u32[]{:S(2)}) collective-permute-start(bf16[2,128,64]{1,0,2:T(2,128)(2,1)S(1)} %collective-permute-done), channel_id=1, source_target_pairs={{0,30},{2,0},{4,2},{6,4},{8,6},{10,8},{12,10},{14,12},{16,14},{18,... | collective-permute-start | bytes 98312 | tf_op jit(solution)/shard_map/ppermute | solution.py:15
  16.4 4.2 %collective-permute-start.2 = (bf16[2,128,64]{1,0,2:T(2,128)(2,1)S(1)}, bf16[2,128,64]{1,0,2:T(2,128)(2,1)S(1)}, u32[]{:S(2)}, u32[]{:S(2)}) collective-permute-start(bf16[2,128,64]{1,0,2:T(2,128)(2,1)S(1)} %collective-permute-done.1), channel_id=1, source_target_pairs={{0,30},{2,0},{4,2},{6,4},{8,6},{10,8},{12,10},{14,12},{16,14},{18,... | collective-permute-start | bytes 98312 | tf_op jit(solution)/shard_map/ppermute | solution.py:15
  20.6 4.2 %collective-permute-start.3 = (bf16[2,128,64]{1,0,2:T(2,128)(2,1)S(1)}, bf16[2,128,64]{1,0,2:T(2,128)(2,1)S(1)}, u32[]{:S(2)}, u32[]{:S(2)}) collective-permute-start(bf16[2,128,64]{1,0,2:T(2,128)(2,1)S(1)} %collective-permute-done.2), channel_id=1, source_target_pairs={{0,30},{2,0},{4,2},{6,4},{8,6},{10,8},{12,10},{14,12},{16,14},{18,... | collective-permute-start | bytes 98312 | tf_op jit(solution)/shard_map/ppermute | solution.py:15
  24.9 4.2 %collective-permute-start.4 = (bf16[2,128,64]{1,0,2:T(2,128)(2,1)S(1)}, bf16[2,128,64]{1,0,2:T(2,128)(2,1)S(1)}, u32[]{:S(2)}, u32[]{:S(2)}) collective-permute-start(bf16[2,128,64]{1,0,2:T(2,128)(2,1)S(1)} %collective-permute-done.3), channel_id=1, source_target_pairs={{0,30},{2,0},{4,2},{6,4},{8,6},{10,8},{12,10},{14,12},{16,14},{18,... | collective-permute-start | bytes 98312 | tf_op jit(solution)/shard_map/ppermute | solution.py:15
  29.1 4.2 %collective-permute-start.5 = (bf16[2,128,64]{1,0,2:T(2,128)(2,1)S(1)}, bf16[2,128,64]{1,0,2:T(2,128)(2,1)S(1)}, u32[]{:S(2)}, u32[]{:S(2)}) collective-permute-start(bf16[2,128,64]{1,0,2:T(2,128)(2,1)S(1)} %collective-permute-done.4), channel_id=1, source_target_pairs={{0,30},{2,0},{4,2},{6,4},{8,6},{10,8},{12,10},{14,12},{16,14},{18,... | collective-permute-start | bytes 98312 | tf_op jit(solution)/shard_map/ppermute | solution.py:15
  33.3 4.2 %collective-permute-start.6 = (bf16[2,128,64]{1,0,2:T(2,128)(2,1)S(1)}, bf16[2,128,64]{1,0,2:T(2,128)(2,1)S(1)}, u32[]{:S(2)}, u32[]{:S(2)}) collective-permute-start(bf16[2,128,64]{1,0,2:T(2,128)(2,1)S(1)} %collective-permute-done.5), channel_id=1, source_target_pairs={{0,30},{2,0},{4,2},{6,4},{8,6},{10,8},{12,10},{14,12},{16,14},{18,... | collective-permute-start | bytes 98312 | tf_op jit(solution)/shard_map/ppermute | solution.py:15
  37.6 4.2 %collective-permute-start.7 = (bf16[2,128,64]{1,0,2:T(2,128)(2,1)S(1)}, bf16[2,128,64]{1,0,2:T(2,128)(2,1)S(1)}, u32[]{:S(2)}, u32[]{:S(2)}) collective-permute-start(bf16[2,128,64]{1,0,2:T(2,128)(2,1)S(1)} %collective-permute-done.6), channel_id=1, source_target_pairs={{0,30},{2,0},{4,2},{6,4},{8,6},{10,8},{12,10},{14,12},{16,14},{18,... | collective-permute-start | bytes 98312 | tf_op jit(solution)/shard_map/ppermute | solution.py:15
  41.8 4.7 %collective-permute-start.8 = (bf16[2,128,64]{1,0,2:T(2,128)(2,1)S(1)}, bf16[2,128,64]{1,0,2:T(2,128)(2,1)S(1)}, u32[]{:S(2)}, u32[]{:S(2)}) collective-permute-start(bf16[2,128,64]{1,0,2:T(2,128)(2,1)S(1)} %collective-permute-done.7), channel_id=1, source_target_pairs={{0,30},{2,0},{4,2},{6,4},{8,6},{10,8},{12,10},{14,12},{16,14},{18,... | collective-permute-start | bytes 98312 | tf_op jit(solution)/shard_map/ppermute | solution.py:15
  46.5 6.0 %collective-permute-start.9 = (bf16[2,128,64]{1,0,2:T(2,128)(2,1)S(1)}, bf16[2,128,64]{1,0,2:T(2,128)(2,1)S(1)}, u32[]{:S(2)}, u32[]{:S(2)}) collective-permute-start(bf16[2,128,64]{1,0,2:T(2,128)(2,1)S(1)} %collective-permute-done.8), channel_id=1, source_target_pairs={{0,30},{2,0},{4,2},{6,4},{8,6},{10,8},{12,10},{14,12},{16,14},{18,... | collective-permute-start | bytes 98312 | tf_op jit(solution)/shard_map/ppermute | solution.py:15
  52.5 6.0 %collective-permute-start.10 = (bf16[2,128,64]{1,0,2:T(2,128)(2,1)S(1)}, bf16[2,128,64]{1,0,2:T(2,128)(2,1)S(1)}, u32[]{:S(2)}, u32[]{:S(2)}) collective-permute-start(bf16[2,128,64]{1,0,2:T(2,128)(2,1)S(1)} %collective-permute-done.9), channel_id=1, source_target_pairs={{0,30},{2,0},{4,2},{6,4},{8,6},{10,8},{12,10},{14,12},{16,14},{18,... | collective-permute-start | bytes 98312 | tf_op jit(solution)/shard_map/ppermute | solution.py:15
  58.6 6.0 %collective-permute-start.11 = (bf16[2,128,64]{1,0,2:T(2,128)(2,1)S(1)}, bf16[2,128,64]{1,0,2:T(2,128)(2,1)S(1)}, u32[]{:S(2)}, u32[]{:S(2)}) collective-permute-start(bf16[2,128,64]{1,0,2:T(2,128)(2,1)S(1)} %collective-permute-done.10), channel_id=1, source_target_pairs={{0,30},{2,0},{4,2},{6,4},{8,6},{10,8},{12,10},{14,12},{16,14},{18,... | collective-permute-start | bytes 98312 | tf_op jit(solution)/shard_map/ppermute | solution.py:15
  64.6 6.0 %collective-permute-start.12 = (bf16[2,128,64]{1,0,2:T(2,128)(2,1)S(1)}, bf16[2,128,64]{1,0,2:T(2,128)(2,1)S(1)}, u32[]{:S(2)}, u32[]{:S(2)}) collective-permute-start(bf16[2,128,64]{1,0,2:T(2,128)(2,1)S(1)} %collective-permute-done.11), channel_id=1, source_target_pairs={{0,30},{2,0},{4,2},{6,4},{8,6},{10,8},{12,10},{14,12},{16,14},{18,... | collective-permute-start | bytes 98312 | tf_op jit(solution)/shard_map/ppermute | solution.py:15
  70.6 6.0 %collective-permute-start.13 = (bf16[2,128,64]{1,0,2:T(2,128)(2,1)S(1)}, bf16[2,128,64]{1,0,2:T(2,128)(2,1)S(1)}, u32[]{:S(2)}, u32[]{:S(2)}) collective-permute-start(bf16[2,128,64]{1,0,2:T(2,128)(2,1)S(1)} %collective-permute-done.12), channel_id=1, source_target_pairs={{0,30},{2,0},{4,2},{6,4},{8,6},{10,8},{12,10},{14,12},{16,14},{18,... | collective-permute-start | bytes 98312 | tf_op jit(solution)/shard_map/ppermute | solution.py:15
  76.7 7.1 %collective-permute-start.14 = (bf16[2,128,64]{1,0,2:T(2,128)(2,1)S(1)}, bf16[2,128,64]{1,0,2:T(2,128)(2,1)S(1)}, u32[]{:S(2)}, u32[]{:S(2)}) collective-permute-start(bf16[2,128,64]{1,0,2:T(2,128)(2,1)S(1)} %collective-permute-done.13), channel_id=1, source_target_pairs={{0,30},{2,0},{4,2},{6,4},{8,6},{10,8},{12,10},{14,12},{16,14},{18,... | collective-permute-start | bytes 98312 | tf_op jit(solution)/shard_map/ppermute | solution.py:15
  165.8 92.8 %all-reduce.2.cloned.1.call-start = ((), (), s32[]{:S(2)}) async-start(), calls=%async_computation.1 | async-start | bytes 131072 | tf_op jit(solution)/shard_map/psum | solution.py:121
  198.3 61.7 %collective-permute-start.18 = (f32[2,128,64]{1,0,2:T(2,128)S(1)}, f32[2,128,64]{1,0,2:T(2,128)S(1)}, u32[]{:S(2)}, u32[]{:S(2)}) collective-permute-start(f32[2,128,64]{1,0,2:T(2,128)S(1)} %get-tuple-element.170), channel_id=1, source_target_pairs={{0,16},{2,18},{4,20},{6,22},{8,24},{10,26},{12,28},{14,30},{16,0},... | collective-permute-start | bytes 196616 | tf_op jit(solution)/shard_map/ppermute | solution.py:22
  200.8 59.3 %collective-permute-start.17 = (f32[2,128,64]{1,0,2:T(2,128)S(1)}, f32[2,128,64]{1,0,2:T(2,128)S(1)}, u32[]{:S(2)}, u32[]{:S(2)}) collective-permute-start(f32[2,128,64]{1,0,2:T(2,128)S(1)} %get-tuple-element.171), channel_id=1, source_target_pairs={{0,8},{2,10},{4,12},{6,14},{8,0},{10,2},{12,4},{14,6},{16,24},{18,... | collective-permute-start | bytes 196616 | tf_op jit(solution)/shard_map/ppermute | solution.py:22
  222.1 38.0 %collective-permute-start.16 = (f32[2,128,64]{1,0,2:T(2,128)S(1)}, f32[2,128,64]{1,0,2:T(2,128)S(1)}, u32[]{:S(2)}, u32[]{:S(2)}) collective-permute-start(f32[2,128,64]{1,0,2:T(2,128)S(1)} %get-tuple-element.172), channel_id=1, source_target_pairs={{0,4},{2,6},{4,0},{6,2},{8,12},{10,14},{12,8},{14,10},{16,20},{18,... | collective-permute-start | bytes 196616 | tf_op jit(solution)/shard_map/ppermute | solution.py:22
  222.1 38.0 %collective-permute-start.15 = (f32[2,128,64]{1,0,2:T(2,128)S(1)}, f32[2,128,64]{1,0,2:T(2,128)S(1)}, u32[]{:S(2)}, u32[]{:S(2)}) collective-permute-start(f32[2,128,64]{1,0,2:T(2,128)S(1)} %get-tuple-element.169), channel_id=1, source_target_pairs={{0,2},{2,0},{4,6},{6,4},{8,10},{10,8},{12,14},{14,12},{16,18},{18,... | collective-permute-start | bytes 196616 | tf_op jit(solution)/shard_map/ppermute | solution.py:22
  (2 other events, 55.7 us)
Sparse Core Ops, SparseCore 0:
  165.9 10.2 reduce-scatter.1
Sparse Core Ops, SparseCore 1:
  170.3 88.3 all-reduce.1
